TPU v7x, 256 devices: a whole 4x4x8 slice. The times are simulated.
256 devices in a mesh: row: 16 (over y_hi, x, core), col: 16 (over z, y_lo).
Axes of the slice: x: 4, y: 4 (y_hi: 2, y_lo: 2; y = y_hi * 2 + y_lo), z: 8, core: 2. Of those that a mesh axis runs over, the one named last changes fastest.
Arguments:
- attn_context: bfloat16 [8192, 4096], P('row', 'col'), may hold values from -6 to 6
- residual: bfloat16 [8192, 2048], P('row', 'col'), may hold values from -8 to 8
- w_out: bfloat16 [4096, 2048], P('col'), may hold values from -0.09375 to 0.09375
- gain_post: bfloat16 [2048], replicated, may hold values from 0.5 to 1.5
- gain_input: bfloat16 [2048], replicated, may hold values from 0.5 to 1.5
- routes: int32 [8192, 8], P('row'), may hold values from 0 to 127, all different within a row; in each aligned block of 512 rows (0 to 511, 512 to 1023, ...) at most 64 rows name the same one
- router_scores: float32 [8192, 8], P('row'), may hold values from 0.02 to 1
- w_gate: bfloat16 [256, 2048, 384], P(('row', 'col')), may hold values from -0.125 to 0.125
- w_up: bfloat16 [256, 2048, 384], P(('row', 'col')), may hold values from -0.125 to 0.125
- w_down: bfloat16 [256, 384, 2048], P(('row', 'col')), may hold values from -0.21875 to 0.21875
- w_query: bfloat16 [2048, 4096], P(None, 'col'), may hold values from -1 to 1
- w_keyval: bfloat16 [2048, 1024], P(None, 'col'), may hold values from -1 to 1
- segment_ids: int32 [16, 504], P('row'), may hold values from 0 to 3, never falling along the last dimension, each value on 1 to 252 neighbouring positions
- cache_lengths: int32 [128], P('row'), may hold values from 1 to 1024, 65536 in all
- holders: int32 [128], P('row'), may hold values from 0 to 127, each once
- cache_keys: bfloat16 [128, 1024, 512], P('row', 'col'), may hold values from -12 to 12
- cache_values: bfloat16 [128, 1024, 512], P('row', 'col'), may hold values from -12 to 12
Outputs:
- hidden_out: bfloat16 [8192, 2048], P('row', 'col')
- new_cache: bfloat16 [8192, 1024], P('row', 'col')
- attention_out: bfloat16 [8192, 4096], P('row', 'col')
Inputs may be any that keep to these rules, and one draw needn't show every extreme that they name: `routes`: in the 512 rows of one index of row, no expert is named by more than 64 rows, and in every draw some expert is named by exactly 64. `segment_ids`: each prompt has at most 252 rows and one has exactly that many. `cache_lengths`: the lengths sum to 65536 and the largest is 1024. `holders`: each cache entry belongs to exactly one decode row.
All inputs are finite; a program needn't handle non-finite values. No bound on the sum of `cache_lengths` on one device may be relied on, other than what follows from the above.
Results may differ from a plain program's by a relative error of at most 0.0175.
Values may be sent and summed in bfloat16 or wider, within the bound.
A program may use at most 128 MiB of HBM per device.

v0:
```python
import jax
import jax.numpy as jnp
from jax import lax
from jax.sharding import PartitionSpec as P

TOP = 8
QH = 32
KVH = 4
HD = 128
EPSILON = 1e-06
ROPE_THETA = 1000000.0
NEGATIVE = -1e30


def merged_2(value, axis, join):
    pieces = jax.tree.map(lambda part: lax.all_gather(part, axis), value)
    head = jax.tree.map(lambda part: part[0], pieces)
    tail = jax.tree.map(lambda part: part[1:], pieces)
    running, _ = lax.scan(lambda running, share: (join(running, share), None), head, tail)
    return running


def rms_norm(hidden, gain_vector):
    values = hidden.astype(jnp.float32)
    inverse = lax.rsqrt(jnp.mean(values * values, axis=-1, keepdims=True) + EPSILON)
    return (values * inverse * gain_vector.astype(jnp.float32)).astype(jnp.bfloat16)


def rotate(values, positions):
    head_width = values.shape[-1]
    half_width = head_width // 2
    indices = jnp.arange(half_width).astype(jnp.float32)
    inverse = ROPE_THETA ** (-2.0 * indices / head_width)
    angles = positions.astype(jnp.float32)[:, None] * inverse[None, :]
    cosine = jnp.concatenate([jnp.cos(angles), jnp.cos(angles)], axis=-1)[:, None, :]
    sine_part = jnp.concatenate([jnp.sin(angles), jnp.sin(angles)], axis=-1)[:, None, :]
    floats = values.astype(jnp.float32)
    turned = jnp.concatenate([-floats[..., half_width:], floats[..., :half_width]], axis=-1)
    return (floats * cosine + turned * sine_part).astype(jnp.bfloat16)


def segment_positions(segment_rows):
    earlier = jnp.sum((segment_rows[None, :] < segment_rows[:, None]).astype(jnp.int32), axis=1)
    return jnp.arange(segment_rows.shape[0], dtype=jnp.int32) - earlier


def spread_norm(hidden, gain_vector):
    gathered = lax.all_gather(hidden, "col", axis=1, tiled=True)
    return (gathered, rms_norm(gathered, gain_vector))


def join_partials(first, second):
    highest = jnp.maximum(first[0], second[0])
    factor_one = jnp.exp(first[0] - highest)
    factor_two = jnp.exp(second[0] - highest)
    weight_mass = first[1] * factor_one + second[1] * factor_two
    accum_out = first[2] * factor_one[..., None] + second[2] * factor_two[..., None]
    return (highest, weight_mass, accum_out)


def shards(
    attn_context,
    residual,
    w_out,
    gain_post,
    gain_input,
    routes,
    router_scores,
    w_gate,
    w_up,
    w_down,
    w_query,
    w_keyval,
    segment_ids,
    cache_lengths,
    holders,
    cache_keys,
    cache_values,
):
    col_index = lax.axis_index("col")
    col_count = lax.axis_size("col")
    row_count = lax.axis_size("row")
    tok_rows = attn_context.shape[0]
    share_width = residual.shape[1]
    model_width = share_width * col_count
    projected = jnp.dot(attn_context, w_out, preferred_element_type=jnp.float32)
    summed = lax.psum_scatter(projected, "col", scatter_dimension=1, tiled=True)
    hidden_mid = (residual.astype(jnp.float32) + summed).astype(jnp.bfloat16)
    full_mid, normed = spread_norm(hidden_mid, gain_post)
    group_width = col_count // 2
    expert_count = row_count * group_width
    capacity = 2 * tok_rows * TOP // expert_count
    route_weight = router_scores / jnp.sum(router_scores, axis=1, keepdims=True)
    matching = routes % group_width == col_index // 2
    target = routes // group_width
    dest_ids = jnp.arange(row_count, dtype=jnp.int32)
    hitting = matching[:, :, None] & (target[:, :, None] == dest_ids[None, None, :])
    sent_flag = jnp.sum(hitting.astype(jnp.int32), axis=1)
    sent_weight = jnp.sum(jnp.where(hitting, route_weight[:, :, None], 0.0), axis=1)
    place = jnp.cumsum(sent_flag, axis=0) - sent_flag
    dest_or_drop = jnp.where(sent_flag > 0, dest_ids[None, :], row_count)
    row_ids = jnp.broadcast_to(
        jnp.arange(tok_rows, dtype=jnp.int32)[:, None], (tok_rows, row_count)
    )
    slot_rows = (
        jnp.full((row_count, capacity), tok_rows, jnp.int32)
        .at[dest_or_drop, place]
        .set(row_ids, mode="drop")
    )
    slot_weight = (
        jnp.zeros((row_count, capacity), jnp.float32)
        .at[dest_or_drop, place]
        .set(sent_weight, mode="drop")
    )
    padded = jnp.concatenate([normed, jnp.zeros((1, model_width), jnp.bfloat16)], axis=0)
    outgoing = padded[slot_rows]
    gate_local = w_gate[0]
    up_local = w_up[0]
    down_local = w_down[0]
    arrived = lax.all_to_all(outgoing, "row", split_axis=0, concat_axis=0, tiled=True)
    flat_rows = arrived.reshape(-1, arrived.shape[2])
    gate_part = jnp.dot(flat_rows, gate_local, preferred_element_type=jnp.float32)
    up_part = jnp.dot(flat_rows, up_local, preferred_element_type=jnp.float32)
    inner = (jax.nn.silu(gate_part) * up_part).astype(jnp.bfloat16)
    result = jnp.dot(inner, down_local, preferred_element_type=jnp.float32).astype(jnp.bfloat16)
    returned = lax.all_to_all(
        result.reshape(arrived.shape), "row", split_axis=0, concat_axis=0, tiled=True
    )
    weighted = slot_weight[:, :, None] * returned.astype(jnp.float32)
    partial_moe = (
        jnp.zeros((tok_rows, model_width), jnp.float32)
        .at[slot_rows.reshape(-1)]
        .add(weighted.reshape(-1, model_width), mode="drop")
    )
    moe_share = lax.psum_scatter(partial_moe, "col", scatter_dimension=1, tiled=True)
    hidden_out = (hidden_mid.astype(jnp.float32) + moe_share).astype(jnp.bfloat16)
    _, x_in = spread_norm(hidden_out, gain_input)
    heads_local = QH // col_count
    dec_count = cache_lengths.shape[0]
    score_scale = HD ** (-0.5)
    query_local = (
        jnp.dot(x_in, w_query, preferred_element_type=jnp.float32)
        .astype(jnp.bfloat16)
        .reshape(tok_rows, heads_local, HD)
    )
    keyval_local = jnp.dot(x_in, w_keyval, preferred_element_type=jnp.float32).astype(jnp.bfloat16)
    position = jnp.concatenate([cache_lengths, segment_positions(segment_ids[0])], axis=0)
    query_rot = rotate(query_local, position)
    dec_query = query_rot[:dec_count].reshape(dec_count, heads_local * HD)
    keyval_all, payload = (
        lax.all_gather(keyval_local, "col", axis=1, tiled=True),
        lax.all_gather(dec_query, "col", axis=1, tiled=True),
    )
    keyval_heads = keyval_all.reshape(tok_rows, KVH, 2, HD)
    key_rot = rotate(keyval_heads[:, :, 0, :], position)
    value_rows = keyval_heads[:, :, 1, :]
    cache_full = jnp.stack([key_rot, value_rows], axis=2).reshape(tok_rows, 2 * KVH * HD)
    cache_share = cache_full.shape[1] // col_count
    new_cache = lax.dynamic_slice_in_dim(cache_full, col_index * cache_share, cache_share, 1)
    head_kv = col_index * heads_local // (QH // KVH)
    my_keys = lax.dynamic_index_in_dim(key_rot, head_kv, 1, keepdims=False)
    my_values = lax.dynamic_index_in_dim(value_rows, head_kv, 1, keepdims=False)
    prompt_query = query_rot[dec_count:]
    prompt_keys = my_keys[dec_count:]
    prompt_values = my_values[dec_count:]
    prompt_rows = prompt_query.shape[0]
    scores = (
        jnp.einsum("ihd,jd->hij", prompt_query, prompt_keys, preferred_element_type=jnp.float32)
        * score_scale
    )
    ordinal = jnp.arange(prompt_rows)
    segment_rows = segment_ids[0]
    allowed = (segment_rows[:, None] == segment_rows[None, :]) & (
        ordinal[None, :] <= ordinal[:, None]
    )
    scores = jnp.where(allowed[None, :, :], scores, NEGATIVE)
    highest = jnp.max(scores, axis=-1, keepdims=True)
    exponent = jnp.exp(scores - highest)
    probability = (exponent / jnp.sum(exponent, axis=-1, keepdims=True)).astype(jnp.bfloat16)
    prompt_out = jnp.einsum(
        "hij,jd->ihd", probability, prompt_values, preferred_element_type=jnp.float32
    )
    prompt_out = prompt_out.astype(jnp.bfloat16).reshape(prompt_rows, heads_local * HD)
    holder_dev = holders // dec_count
    holder_slot = holders % dec_count
    outbox = (
        jnp.zeros((row_count, dec_count, payload.shape[1]), jnp.bfloat16)
        .at[holder_dev, holder_slot]
        .set(payload)
    )
    length_box = (
        jnp.zeros((row_count, dec_count), jnp.int32).at[holder_dev, holder_slot].set(cache_lengths)
    )
    inbox, length_in = (
        lax.all_to_all(outbox, "row", split_axis=0, concat_axis=0, tiled=True),
        lax.all_to_all(length_box, "row", split_axis=0, concat_axis=0, tiled=True),
    )
    slot_query = jnp.sum(inbox.astype(jnp.float32), axis=0).astype(jnp.bfloat16)
    slot_length = jnp.sum(length_in, axis=0)
    span_len = cache_keys.shape[1]
    span_start = col_index * span_len
    grouped = slot_query.reshape(dec_count, KVH, QH // KVH, HD)
    held_keys = cache_keys.reshape(dec_count, span_len, KVH, HD)
    held_values = cache_values.reshape(dec_count, span_len, KVH, HD).astype(jnp.float32)
    held_scores = (
        jnp.einsum("sgqd,stgd->sgqt", grouped, held_keys, preferred_element_type=jnp.float32)
        * score_scale
    )
    valid = ((span_start + jnp.arange(span_len))[None, :] < slot_length[:, None])[:, None, None, :]
    held_scores = jnp.where(valid, held_scores, NEGATIVE)
    score_top = jnp.max(held_scores, axis=-1)
    held_exp = jnp.where(valid, jnp.exp(held_scores - score_top[..., None]), 0.0)
    weight_mass = jnp.sum(held_exp, axis=-1).reshape(dec_count, QH)
    accum_out = jnp.einsum(
        "sgqt,stgd->sgqd", held_exp, held_values, precision=lax.Precision.HIGHEST
    ).reshape(dec_count, QH, HD)
    score_top = score_top.reshape(dec_count, QH)
    merged = merged_2((score_top, weight_mass, accum_out), "col", join_partials)
    part_top = lax.dynamic_slice_in_dim(merged[0], col_index * heads_local, heads_local, 1)
    part_mass = lax.dynamic_slice_in_dim(merged[1], col_index * heads_local, heads_local, 1)
    part_accum = lax.dynamic_slice_in_dim(merged[2], col_index * heads_local, heads_local, 1)
    reply_top = jnp.broadcast_to(part_top[None], (row_count,) + part_top.shape)
    reply_mass = jnp.broadcast_to(part_mass[None], (row_count,) + part_mass.shape)
    reply_accum = jnp.broadcast_to(part_accum[None], (row_count,) + part_accum.shape)
    back_top, back_mass, back_accum = (
        lax.all_to_all(reply_top, "row", split_axis=0, concat_axis=0, tiled=True),
        lax.all_to_all(reply_mass, "row", split_axis=0, concat_axis=0, tiled=True),
        lax.all_to_all(reply_accum, "row", split_axis=0, concat_axis=0, tiled=True),
    )
    remote_top = back_top[holder_dev, holder_slot]
    remote_mass = back_mass[holder_dev, holder_slot]
    remote_accum = back_accum[holder_dev, holder_slot]
    own_query = query_rot[:dec_count].astype(jnp.float32)
    own_key = my_keys[:dec_count].astype(jnp.float32)
    own_value = my_values[:dec_count].astype(jnp.float32)
    own_score = (
        jnp.einsum("shd,sd->sh", own_query, own_key, precision=lax.Precision.HIGHEST) * score_scale
    )
    final_top = jnp.maximum(remote_top, own_score)
    remote_factor = jnp.exp(remote_top - final_top)
    own_factor = jnp.exp(own_score - final_top)
    numerator = (
        remote_accum * remote_factor[..., None] + own_factor[..., None] * own_value[:, None, :]
    )
    denominator = remote_mass * remote_factor + own_factor
    decode_out = (
        (numerator / denominator[..., None])
        .reshape(dec_count, heads_local * HD)
        .astype(jnp.bfloat16)
    )
    attention_out = jnp.concatenate([decode_out, prompt_out], axis=0)
    return (hidden_out, new_cache, attention_out)


def solution(mesh):
    return jax.shard_map(
        shards,
        mesh=mesh,
        in_specs=(
            P("row", "col"),
            P("row", "col"),
            P("col", None),
            P(),
            P(),
            P("row", None),
            P("row", None),
            P(("row", "col"), None, None),
            P(("row", "col"), None, None),
            P(("row", "col"), None, None),
            P(None, "col"),
            P(None, "col"),
            P("row", None),
            P("row"),
            P("row"),
            P("row", "col", None),
            P("row", "col", None),
        ),
        out_specs=(P("row", "col"), P("row", "col"), P("row", "col")),
        check_vma=False,
    )
```

profile of v0, /device:TPU:1, one launch (start us, length us, event | category | flops | bytes accessed | tf_op | source)
XLA Modules:
  0.0 781.5 jit_solution(6182529554980959249)
XLA Ops:
  7.2 4.1 fusion.103
  11.4 102.1 %reduce-scatter.3.cloned.1.call-done = f32[512,128]{1,0:T(8,128)} async-done(((f32[512,2048]{1,0:T(8,128)}), f32[512,128]{1,0:T(8,128)}) %reduce-scatter.3.cloned.1.call-update) | async-done | bytes 262160 | tf_op jit(solution)/shard_map/reduce_scatter | solution.py:87
  117.4 30.4 %scatter_custom_fusion.3 = s32[1024]{0:T(1024)S(1)} fusion(s32[8192]{0:T(1024)S(1)} %reshape.353, s32[8192]{0:T(1024)S(1)} %reshape.355, s32[]{:T(128)} %constant.121.clone.1), kind=kCustom, calls=%fused_computation.150 | custom fusion | bytes 4100
  148.0 42.8 %all-gather.5.cloned.1.call-done = bf16[512,2048]{1,0:T(8,128)(2,1)} async-done(((bf16[512,128]{1,0:T(8,128)(2,1)}), bf16[512,2048]{1,0:T(8,128)(2,1)}) %all-gather.5.cloned.1.call-update) | async-done | bytes 2097168 | tf_op jit(solution)/shard_map/all_gather | solution.py:48
  195.0 10.7 %gather_fusion = bf16[1024,2048]{1,0:T(8,128)(2,1)} fusion(bf16[513,2048]{1,0:T(8,128)(2,1)} %concatenate.52, s32[1024]{0:T(1024)S(1)} %broadcast_clamp_fusion), kind=kCustom, calls=%fused_computation | custom fusion | bytes 8392704 | tf_op jit(solution)/shard_map/gather | solution.py:116
  205.7 68.1 %all_to_all.39 = bf16[16,64,2048]{2,1,0:T(8,128)(2,1)S(1)} all-to-all(bf16[16,64,2048]{2,1,0:T(8,128)(2,1)} %bitcast.177), channel_id=1, replica_groups=mesh['row'=16,'col'=16] {'row'}, dimensions={0} | all-to-all | bytes 8388608 | tf_op jit(solution)/shard_map/all_to_all | solution.py:120
  275.9 3.6 fusion.16
  279.4 7.8 convolution_convert_fusion
  287.2 5.5 all-to-all-start.1
  293.2 30.6 %scatter_custom_fusion.4 = f32[1024]{0:T(1024)S(1)} fusion(s32[8192]{0:T(1024)S(1)} %reshape.353, f32[8192]{0:T(1024)S(1)} %reshape.361, f32[]{:T(128)} %constant.120.clone.1), kind=kCustom, calls=%fused_computation.148 | custom fusion | bytes 4100
  323.9 24.7 %all-to-all-done.1 = bf16[16,64,2048]{2,1,0:T(8,128)(2,1)} async-done(((bf16[16,64,2048]{2,1,0:T(8,128)(2,1)}), bf16[16,64,2048]{2,1,0:T(8,128)(2,1)}, u32[]{:S(2)}, u32[]{:S(2)}) %all-to-all-start.1) | async-done | bytes 4194336 | tf_op jit(solution)/shard_map/all_to_all | solution.py:126
  348.5 6.0 convert_multiply_fusion
  354.5 16.9 %scatter_custom_fusion = f32[512,2048]{1,0:T(8,128)} fusion(s32[1024]{0:T(1024)S(1)} %bitcast.191, f32[1024,2048]{1,0:T(8,128)} %bitcast.178, f32[]{:T(128)} %constant.120.clone.1), kind=kCustom, calls=%fused_computation.30 | custom fusion | flops 2097152 | bytes 4194816 | tf_op jit(solution)/shard_map/scatter-add | solution.py:133
  371.5 98.3 %reduce-scatter.5.cloned.1.call-done = f32[512,128]{1,0:T(8,128)} async-done(((f32[512,2048]{1,0:T(8,128)}), f32[512,128]{1,0:T(8,128)}) %reduce-scatter.5.cloned.1.call-update) | async-done | bytes 262160 | tf_op jit(solution)/shard_map/reduce_scatter | solution.py:135
  473.1 9.1 %all-to-all-start.2 = ((s32[16,1,8]{2,1,0:T(1,128)}), s32[16,1,8]{2,1,0:T(1,128)S(1)}, u32[]{:S(2)}, u32[]{:S(2)}) async-start(s32[16,1,8]{2,1,0:T(1,128)} %copy.82), calls=%async_computation.4 | async-start | bytes 16384 | tf_op jit(solution)/shard_map/all_to_all | solution.py:196
  483.9 63.3 %all-gather.7.cloned.1.call-done = bf16[512,2048]{1,0:T(8,128)(2,1)} async-done(((bf16[512,128]{1,0:T(8,128)(2,1)}), bf16[512,2048]{1,0:T(8,128)(2,1)}) %all-gather.7.cloned.1.call-update) | async-done | bytes 2097168 | tf_op jit(solution)/shard_map/all_gather | solution.py:48
  554.2 24.0 %all_gather.24 = bf16[8,4096]{1,0:T(8,128)(2,1)S(1)} all-gather(bf16[8,256]{1,0:T(8,128)(2,1)S(1)} %get-tuple-element.84), channel_id=1, replica_groups=mesh['row'=16,'col'=16] {'col'}, dimensions={1}, use_global_device_ids=true | all-gather | bytes 69632 | tf_op jit(solution)/shard_map/all_gather | solution.py:152
  579.2 3.3 scatter_fusion.1
  582.6 25.2 %all-to-all-start.3 = ((bf16[16,8,4096]{2,1,0:T(8,128)(2,1)}), bf16[16,8,4096]{2,1,0:T(8,128)(2,1)S(1)}, u32[]{:S(2)}, u32[]{:S(2)}) async-start(bf16[16,8,4096]{2,1,0:T(8,128)(2,1)} %scatter_fusion.1), calls=%async_computation.5 | async-start | bytes 2097152 | tf_op jit(solution)/shard_map/all_to_all | solution.py:195
  607.9 18.1 %all-to-all-done.3 = bf16[16,8,4096]{2,1,0:T(8,128)(2,1)S(1)} async-done(((bf16[16,8,4096]{2,1,0:T(8,128)(2,1)}), bf16[16,8,4096]{2,1,0:T(8,128)(2,1)S(1)}, u32[]{:S(2)}, u32[]{:S(2)}) %all-to-all-start.3) | async-done | bytes 1048608 | tf_op jit(solution)/shard_map/all_to_all | solution.py:195
  629.2 23.4 %all_gather.26 = f32[16,8,32]{2,1,0:T(8,128)S(1)} all-gather(f32[1,8,32]{2,1,0:T(8,128)S(1)} %all_gather_reshape.10), channel_id=1, replica_groups=mesh['row'=16,'col'=16] {'col'}, dimensions={0}, use_global_device_ids=true | all-gather | bytes 17408 | tf_op jit(solution)/shard_map/all_gather | solution.py:16
  652.7 27.2 %all_gather.25 = f32[16,8,32]{2,1,0:T(8,128)S(1)} all-gather(f32[1,8,32]{2,1,0:T(8,128)S(1)} %all_gather_reshape.9), channel_id=1, replica_groups=mesh['row'=16,'col'=16] {'col'}, dimensions={0}, use_global_device_ids=true | all-gather | bytes 17408 | tf_op jit(solution)/shard_map/all_gather | solution.py:16
  686.6 3.1 fusion.20
  693.9 10.1 %all-gather.11.cloned.1.call-done = f32[16,8,32,128]{3,2,1,0:T(8,128)} async-done(((f32[1,8,32,128]{3,2,1,0:T(8,128)}), f32[16,8,32,128]{3,2,1,0:T(8,128)}) %all-gather.11.cloned.1.call-update) | async-done | bytes 2097168 | tf_op jit(solution)/shard_map/all_gather | solution.py:16
  704.0 3.0 slice.119
  708.0 16.8 %while.14 = (s32[]{:T(128)}, f32[8,32]{1,0:T(8,128)S(1)}, f32[8,32]{1,0:T(8,128)S(1)}, f32[8,32,128]{2,1,0:T(8,128)S(1)}, f32[15,8,32]{2,1,0:T(8,128)S(1)}, /*in...) while((s32[]{:T(128)}, f32[8,32]{1,0:T(8,128)S(1)}, f32[8,32]{1,0:T(8,128)S(1)}, ...), condition=%wide.region_20.21_spmd, body=%wide.region_19.20_spmd.sunk | while | flops 99842 | bytes 403549 | solution.py:19
  725.6 16.2 %all-to-all-start.5 = ((f32[16,8,2]{1,2,0:T(2,128)}), f32[16,8,2]{1,2,0:T(2,128)S(1)}, u32[]{:S(2)}, u32[]{:S(2)}) async-start(f32[16,8,2]{1,2,0:T(2,128)} %broadcast_in_dim.100), calls=%async_computation.7 | async-start | bytes 32768 | tf_op jit(solution)/shard_map/all_to_all | solution.py:226
  742.0 7.1 all-to-all-done.5
  749.7 3.7 all-to-all-start.6
  754.2 6.6 all-to-all-done.6
  761.5 3.7 all-to-all-start.4
  765.9 6.9 all-to-all-done.4
  (201 shorter events, 60.8 us)
Async XLA Ops:
  7.2 272.2 %copy-start = (bf16[1,384,2048]{2,1,0:T(8,128)(2,1)S(1)}, bf16[1,384,2048]{2,1,0:T(8,128)(2,1)}, u32[]{:S(2)}) copy-start(bf16[1,384,2048]{2,1,0:T(8,128)(2,1)} %param.28) | copy-start | bytes 4718596
  7.2 106.3 %reduce-scatter.3.cloned.1.call-start = ((), (), s32[]{:S(2)}) async-start(), calls=%async_computation.9 | async-start | bytes 4456448 | tf_op jit(solution)/shard_map/reduce_scatter | solution.py:87
  11.3 102.2 %copy-start.11 = (bf16[512,128]{1,0:T(8,128)(2,1)S(1)}, bf16[512,128]{1,0:T(8,128)(2,1)}, u32[]{:S(2)}) copy-start(bf16[512,128]{1,0:T(8,128)(2,1)} %param.20) | copy-start | bytes 393220
  11.3 103.8 %copy-start.12 = (s32[512,8]{0,1:T(8,128)S(1)}, s32[512,8]{0,1:T(8,128)}, u32[]{:S(2)}) copy-start(s32[512,8]{0,1:T(8,128)} %param.24) | copy-start | bytes 49156
  11.3 105.5 %copy-start.19 = (s32[2]{0:T(128)S(1)}, s32[2]{0:T(128)}, u32[]{:S(2)}) copy-start(s32[2]{0:T(128)} %constant.155) | copy-start | bytes 28
  11.3 105.6 %copy-start.18 = (s32[2]{0:T(128)S(1)}, s32[2]{0:T(128)}, u32[]{:S(2)}) copy-start(s32[2]{0:T(128)} %constant.158) | copy-start | bytes 28
  11.3 136.7 %copy-start.15 = (bf16[2048]{0:T(1024)(128)(2,1)S(1)}, bf16[2048]{0:T(1024)(128)(2,1)}, u32[]{:S(2)}) copy-start(bf16[2048]{0:T(1024)(128)(2,1)} %param.22) | copy-start | bytes 12292
  11.3 179.4 %all-gather.5.cloned.1.call-start = ((), (), s32[]{:S(2)}) async-start(), calls=%async_computation.10 | async-start | bytes 2228224 | tf_op jit(solution)/shard_map/all_gather | solution.py:48
  205.7 70.1 %copy-start.20 = (bf16[1,2048,384]{2,1,0:T(8,128)(2,1)S(1)}, bf16[1,2048,384]{2,1,0:T(8,128)(2,1)}, u32[]{:S(2)}) copy-start(bf16[1,2048,384]{2,1,0:T(8,128)(2,1)} %param.26) | copy-start | bytes 4718596
  287.2 5.6 copy-start.13
  287.2 61.3 %all-to-all-start.1 = ((bf16[16,64,2048]{2,1,0:T(8,128)(2,1)}), bf16[16,64,2048]{2,1,0:T(8,128)(2,1)}, u32[]{:S(2)}, u32[]{:S(2)}) async-start(bf16[16,64,2048]{2,1,0:T(8,128)(2,1)} %bitcast.179), calls=%async_computation.2 | async-start | bytes 8388608 | tf_op jit(solution)/shard_map/all_to_all | solution.py:126
  292.7 177.1 %reduce-scatter.5.cloned.1.call-start = ((), (), s32[]{:S(2)}) async-start(), calls=%async_computation.11 | async-start | bytes 4456448 | tf_op jit(solution)/shard_map/reduce_scatter | solution.py:135
  371.4 98.4 %copy-start.7 = (bf16[512,128]{1,0:T(8,128)(2,1)S(1)}, bf16[512,128]{1,0:T(8,128)(2,1)}, u32[]{:S(2)}) copy-start(bf16[512,128]{1,0:T(8,128)(2,1)} %add_convert_fusion.1) | copy-start | bytes 393220
  371.4 100.1 %copy-start.25 = (s32[8]{0:T(128)S(1)}, s32[8]{0:T(128)}, u32[]{:S(2)}) copy-start(s32[8]{0:T(128)} %param.33) | copy-start | bytes 100
  371.4 100.1 %copy-start.17 = (s32[8]{0:T(128)S(1)}, s32[8]{0:T(128)}, u32[]{:S(2)}) copy-start(s32[8]{0:T(128)} %param.32) | copy-start | bytes 100
  371.4 111.0 %copy-start.16 = (bf16[2048]{0:T(1024)(128)(2,1)S(1)}, bf16[2048]{0:T(1024)(128)(2,1)}, u32[]{:S(2)}) copy-start(bf16[2048]{0:T(1024)(128)(2,1)} %param.23) | copy-start | bytes 12292
  371.4 111.0 %copy-start.14 = (s32[1,504]{1,0:T(1,128)S(1)}, s32[1,504]{1,0:T(1,128)}, u32[]{:S(2)}) copy-start(s32[1,504]{1,0:T(1,128)} %param.31) | copy-start | bytes 6052
  371.5 175.8 %all-gather.7.cloned.1.call-start = ((), (), s32[]{:S(2)}) async-start(), calls=%async_computation.12 | async-start | bytes 2228224 | tf_op jit(solution)/shard_map/all_gather | solution.py:48
  472.4 77.1 %copy-start.24 = (bf16[2048,64]{0,1:T(8,128)(2,1)S(1)}, bf16[2048,64]{0,1:T(8,128)(2,1)}, u32[]{:S(2)}) copy-start(bf16[2048,64]{0,1:T(8,128)(2,1)} %param.30) | copy-start | bytes 786436
  473.1 109.5 %all-to-all-start.2 = ((s32[16,1,8]{2,1,0:T(1,128)}), s32[16,1,8]{2,1,0:T(1,128)S(1)}, u32[]{:S(2)}, u32[]{:S(2)}) async-start(s32[16,1,8]{2,1,0:T(1,128)} %copy.82), calls=%async_computation.4 | async-start | bytes 16384 | tf_op jit(solution)/shard_map/all_to_all | solution.py:196
  482.2 197.7 %all-gather.9.cloned.1.call-start = ((), (), s32[]{:S(2)}) async-start(), calls=%async_computation.13 | async-start | bytes 1114112 | tf_op jit(solution)/shard_map/all_gather | solution.py:151
  579.2 46.9 %copy-start.8 = (bf16[8,64,512]{2,1,0:T(8,128)(2,1)S(1)}, bf16[8,64,512]{2,1,0:T(8,128)(2,1)}, u32[]{:S(2)}) copy-start(bf16[8,64,512]{2,1,0:T(8,128)(2,1)} %param.34) | copy-start | bytes 1572868
  582.6 44.1 %copy-start.23 = (bf16[8,64,512]{2,1,0:T(8,128)(2,1)S(1)}, bf16[8,64,512]{2,1,0:T(8,128)(2,1)}, u32[]{:S(2)}) copy-start(bf16[8,64,512]{2,1,0:T(8,128)(2,1)} %param.35) | copy-start | bytes 1572868
  582.6 43.4 %all-to-all-start.3 = ((bf16[16,8,4096]{2,1,0:T(8,128)(2,1)}), bf16[16,8,4096]{2,1,0:T(8,128)(2,1)S(1)}, u32[]{:S(2)}, u32[]{:S(2)}) async-start(bf16[16,8,4096]{2,1,0:T(8,128)(2,1)} %scatter_fusion.1), calls=%async_computation.5 | async-start | bytes 2097152 | tf_op jit(solution)/shard_map/all_to_all | solution.py:195
  607.8 96.3 %all-gather.11.cloned.1.call-start = ((), (), s32[]{:S(2)}) async-start(), calls=%async_computation.14 | async-start | bytes 2228224 | tf_op jit(solution)/shard_map/all_gather | solution.py:16
  652.7 29.8 %copy-start.9 = (f32[16,8,32]{2,1,0:T(8,128)}, f32[16,8,32]{2,1,0:T(8,128)S(1)}, u32[]{:S(2)}) copy-start(f32[16,8,32]{2,1,0:T(8,128)S(1)} %all_gather.26) | copy-start | bytes 49156
  693.9 14.0 %slice-start = ((f32[16,8,32]{2,1,0:T(8,128)}), f32[15,8,32]{2,1,0:T(8,128)S(1)}, s32[]{:S(2)}) async-start(f32[16,8,32]{2,1,0:T(8,128)} %copy-done.9), calls=%async_computation.15 | async-start | bytes 122880 | tf_op jit(solution)/shard_map/slice | solution.py:18
  693.9 14.1 %slice-start.1 = ((f32[16,8,32]{2,1,0:T(8,128)}), f32[15,8,32]{2,1,0:T(8,128)S(1)}, s32[]{:S(2)}) async-start(f32[16,8,32]{2,1,0:T(8,128)} %copy-done.10), calls=%async_computation.16 | async-start | bytes 122880 | tf_op jit(solution)/shard_map/slice | solution.py:18
  708.0 66.6 %copy-start.1 = (bf16[1,384,2048]{2,1,0:T(8,128)(2,1)S(1)}, bf16[1,384,2048]{2,1,0:T(8,128)(2,1)}, u32[]{:S(2)}) copy-start(bf16[1,384,2048]{2,1,0:T(8,128)(2,1)} %param.28) | copy-start | bytes 4718596
  725.6 23.5 %all-to-all-start.5 = ((f32[16,8,2]{1,2,0:T(2,128)}), f32[16,8,2]{1,2,0:T(2,128)S(1)}, u32[]{:S(2)}, u32[]{:S(2)}) async-start(f32[16,8,2]{1,2,0:T(2,128)} %broadcast_in_dim.100), calls=%async_computation.7 | async-start | bytes 32768 | tf_op jit(solution)/shard_map/all_to_all | solution.py:226
  749.7 11.0 %all-to-all-start.6 = ((f32[16,8,2]{1,2,0:T(2,128)}), f32[16,8,2]{1,2,0:T(2,128)S(1)}, u32[]{:S(2)}, u32[]{:S(2)}) async-start(f32[16,8,2]{1,2,0:T(2,128)} %broadcast_in_dim.101), calls=%async_computation.8 | async-start | bytes 32768 | tf_op jit(solution)/shard_map/all_to_all | solution.py:227
  761.5 11.4 %all-to-all-start.4 = ((f32[16,8,2,128]{3,2,1,0:T(2,128)}), f32[16,8,2,128]{3,2,1,0:T(2,128)S(1)}, u32[]{:S(2)}, u32[]{:S(2)}) async-start(f32[16,8,2,128]{3,2,1,0:T(2,128)} %broadcast_in_dim.99), calls=%async_computation.6 | async-start | bytes 262144 | tf_op jit(solution)/shard_map/all_to_all | solution.py:228
  (8 other events, 19.5 us)
Sparse Core Ops, SparseCore 0:
  11.5 101.9 reduce-scatter.2
  115.7 74.9 all-gather.4
  371.6 98.2 reduce-scatter.4
  472.0 75.2 all-gather.6
  551.1 76.3 all-gather.8
  629.1 74.8 all-gather.10
where the time goes:
time: 783 us; the launch traced here: 781 us
  waiting for transfers between devices  380 us (49%)
  blocking collectives  143 us (18%)
  local copies, waits for them, and re-layouts  97.3 us (12%)
  starting transfers between devices  63.8 us (8%)
  other arithmetic  55.6 us (7%)
  matrix products  26.9 us (3%)
  between operations  14.7 us (2%)
    all_gather x2, waiting for transfers between devices, spread_norm(): gathered = lax.all_gather(hidden, 'col', axis=1, tiled=True)  106 us
    reduce_scatter x1, waiting for transfers between devices, shards(): summed = lax.psum_scatter(projected, 'col', scatter_dimension=1, tiled=True)  102 us
    reduce_scatter x1, waiting for transfers between devices, shards(): lax.psum_scatter(partial_moe, 'col', scatter_dimension=1, tiled=True)  98.3 us
    all_to_all x1, blocking collectives, shards(): lax.all_to_all(outgoing, 'row', split_axis=0, concat_axis=0, tiled=True)  68.1 us
    unnamed x59, local copies, waits for them, and re-layouts  66.1 us
    all_gather x2, blocking collectives, merged_2(): pieces = jax.tree.map(lambda part: lax.all_gather(part, axis), value)  50.6 us
    all_to_all x1, starting transfers between devices, shards(): lax.all_to_all(outbox, 'row', split_axis=0, concat_axis=0, tiled=True)  25.2 us
    all_to_all x1, waiting for transfers between devices, shards(): lax.all_to_all(result.reshape(arrived.shape), 'row', split_axis=0, concat...  24.7 us
  transfers between devices with their start and end apart: 12, of which 10 were waited for; matrix products, arithmetic and copies ran while one was open for 12% of the time, Pallas kernels for 0%

commit v1 on v0

--- a/solution.py
+++ b/solution.py
@@ -1,3 +1,4 @@
+import functools
 import jax
 import jax.numpy as jnp
 from jax import lax
@@ -10,6 +11,16 @@
 EPSILON = 1e-06
 ROPE_THETA = 1000000.0
 NEGATIVE = -1e30
+
+
+def track_slot_in(chunk, a_name):
+    d_next = jnp.stack([chunk for _ in range(lax.axis_size(a_name))])
+    f_now = lax.all_to_all(d_next, axis_name=a_name, split_axis=0, concat_axis=0)
+    mixed_arr = jnp.concatenate(f_now, axis=1)
+    return mixed_arr
+
+
+clear_rings = functools.partial(track_slot_in, a_name="col")
 
 
 def merged_2(value, axis, join):
@@ -45,7 +56,7 @@
 
 
 def spread_norm(hidden, gain_vector):
-    gathered = lax.all_gather(hidden, "col", axis=1, tiled=True)
+    gathered = clear_rings(hidden)
     return (gathered, rms_norm(gathered, gain_vector))
 
 

time: 783 us -> 737 us (0.941)
  waiting for transfers between devices: 380 us -> 329 us
  blocking collectives: 143 us -> 135 us
    all_gather x2 -> x0, waiting for transfers between devices: 106 us -> none  [spread_norm(): gathered = lax.all_gather(hidden, 'col', axis=1, tiled=True)]
    all_to_all x0 -> x2, waiting for transfers between devices: none -> 60.1 us  [track_slot_in(): lax.all_to_all(d_next, axis_name=a_name, split_axis=0, concat_axis=0)]
    all_to_all x0 -> x2, starting transfers between devices: none -> 14.2 us  [track_slot_in(): lax.all_to_all(d_next, axis_name=a_name, split_axis=0, concat_axis=0)]
    all_to_all x1, starting transfers between devices: 25.2 us -> 14.1 us  [shards(): lax.all_to_all(outbox, 'row', split_axis=0, concat_axis=0, tiled=True)]
    unnamed x59 -> x53, local copies, waits for them, and re-layouts: 66.1 us -> 67.3 us
  transfers between devices with their start and end apart: 12 -> 12, of which waited for: 10 -> 10; matrix products, arithmetic and copies ran while one was open for 12% -> 13% of each run, Pallas kernels for 0% -> 0%
where the time goes in v1:
time: 737 us; the launch traced here: 735 us
  waiting for transfers between devices  329 us (45%)
  blocking collectives  135 us (18%)
  local copies, waits for them, and re-layouts  102 us (14%)
  starting transfers between devices  69 us (9%)
  other arithmetic  57.8 us (8%)
  matrix products  28.3 us (4%)
  between operations  14.4 us (2%)
    reduce_scatter x1, waiting for transfers between devices, shards(): summed = lax.psum_scatter(projected, 'col', scatter_dimension=1, tiled=True)  102 us
    reduce_scatter x1, waiting for transfers between devices, shards(): lax.psum_scatter(partial_moe, 'col', scatter_dimension=1, tiled=True)  95.6 us
    unnamed x53, local copies, waits for them, and re-layouts  67.3 us
    all_to_all x1, blocking collectives, shards(): lax.all_to_all(outgoing, 'row', split_axis=0, concat_axis=0, tiled=True)  60.9 us
    all_to_all x2, waiting for transfers between devices, track_slot_in(): lax.all_to_all(d_next, axis_name=a_name, split_axis=0, concat_axis=0)  60.1 us
    all_gather x2, blocking collectives, merged_2(): pieces = jax.tree.map(lambda part: lax.all_gather(part, axis), value)  50.2 us
    all_to_all x1, waiting for transfers between devices, shards(): lax.all_to_all(result.reshape(arrived.shape), 'row', split_axis=0, concat...  24.7 us
    all_gather x1, blocking collectives, shards(): lax.all_gather(dec_query, 'col', axis=1, tiled=True)  23.5 us
  transfers between devices with their start and end apart: 12, of which 10 were waited for; matrix products, arithmetic and copies ran while one was open for 13% of the time, Pallas kernels for 0%

profile of v1, /device:TPU:1, one launch (start us, length us, event | category | flops | bytes accessed | tf_op | source)
XLA Modules:
  0.0 735.5 jit_solution(9118210504465858847)
XLA Ops:
  7.2 4.1 fusion.100
  11.3 102.1 %reduce-scatter.3.cloned.1.call-done = f32[512,128]{1,0:T(8,128)} async-done(((f32[512,2048]{1,0:T(8,128)}), f32[512,128]{1,0:T(8,128)}) %reduce-scatter.3.cloned.1.call-update) | async-done | bytes 262160 | tf_op jit(solution)/shard_map/reduce_scatter | solution.py:98
  116.1 7.1 all-to-all-start
  125.5 30.4 %scatter_custom_fusion.3 = s32[1024]{0:T(1024)S(1)} fusion(s32[8192]{0:T(1024)S(1)} %reshape.367, s32[8192]{0:T(1024)S(1)} %reshape.369, s32[]{:T(128)} %constant.121.clone.1), kind=kCustom, calls=%fused_computation.150 | custom fusion | bytes 4100
  156.1 15.2 %all-to-all-done = bf16[16,512,128]{2,1,0:T(8,128)(2,1)} async-done(((bf16[16,512,128]{2,1,0:T(8,128)(2,1)}), bf16[16,512,128]{2,1,0:T(8,128)(2,1)}, u32[]{:S(2)}, u32[]{:S(2)}) %all-to-all-start) | async-done | bytes 2097184 | tf_op jit(solution)/shard_map/all_to_all | solution.py:18
  177.0 10.7 %gather_fusion = bf16[1024,2048]{1,0:T(8,128)(2,1)} fusion(bf16[513,2048]{1,0:T(8,128)(2,1)} %concatenate.52, s32[1024]{0:T(1024)S(1)} %broadcast_clamp_fusion), kind=kCustom, calls=%fused_computation | custom fusion | bytes 8392704 | tf_op jit(solution)/shard_map/gather | solution.py:127
  187.7 60.9 %all_to_all.49 = bf16[16,64,2048]{2,1,0:T(8,128)(2,1)S(1)} all-to-all(bf16[16,64,2048]{2,1,0:T(8,128)(2,1)} %bitcast.197), channel_id=1, replica_groups=mesh['row'=16,'col'=16] {'row'}, dimensions={0} | all-to-all | bytes 8388608 | tf_op jit(solution)/shard_map/all_to_all | solution.py:131
  250.6 3.6 fusion.15
  254.1 9.6 %convolution_convert_fusion = bf16[1024,2048]{1,0:T(8,128)(2,1)} fusion(bf16[1,384,2048]{2,1,0:T(8,128)(2,1)S(1)} %copy-done, f32[1024,384]{1,0:T(8,128)} %fusion.15, bf16[1024,2048]{1,0:T(8,128)(2,1)} %bitcast.201, bf16[1,2048,384]{2,1,0:T(8,128)(2,1)} %param.27), kind=kOutput, calls=%fused_computation.29 | convolution fusion | flops 3225681920 | bytes 13107200 | tf_op jit(solution)/shard_map/dot_general | solution.py:136
  263.7 5.5 all-to-all-start.2
  269.8 30.4 %scatter_custom_fusion.4 = f32[1024]{0:T(1024)S(1)} fusion(s32[8192]{0:T(1024)S(1)} %reshape.367, f32[8192]{0:T(1024)S(1)} %reshape.375, f32[]{:T(128)} %constant.120.clone.1), kind=kCustom, calls=%fused_computation.148 | custom fusion | bytes 4100
  300.3 24.7 %all-to-all-done.2 = bf16[16,64,2048]{2,1,0:T(8,128)(2,1)} async-done(((bf16[16,64,2048]{2,1,0:T(8,128)(2,1)}), bf16[16,64,2048]{2,1,0:T(8,128)(2,1)}, u32[]{:S(2)}, u32[]{:S(2)}) %all-to-all-start.2) | async-done | bytes 4194336 | tf_op jit(solution)/shard_map/all_to_all | solution.py:137
  324.9 6.0 convert_multiply_fusion
  331.0 16.9 %scatter_custom_fusion = f32[512,2048]{1,0:T(8,128)} fusion(s32[1024]{0:T(1024)S(1)} %bitcast.211, f32[1024,2048]{1,0:T(8,128)} %bitcast.198, f32[]{:T(128)} %constant.120.clone.1), kind=kCustom, calls=%fused_computation.30 | custom fusion | flops 2097152 | bytes 4194816 | tf_op jit(solution)/shard_map/scatter-add | solution.py:144
  347.9 95.6 %reduce-scatter.5.cloned.1.call-done = f32[512,128]{1,0:T(8,128)} async-done(((f32[512,2048]{1,0:T(8,128)}), f32[512,128]{1,0:T(8,128)}) %reduce-scatter.5.cloned.1.call-update) | async-done | bytes 262160 | tf_op jit(solution)/shard_map/reduce_scatter | solution.py:146
  446.1 7.0 all-to-all-start.3
  456.3 44.9 %all-to-all-done.3 = bf16[16,512,128]{1,2,0:T(8,128)(2,1)} async-done(((bf16[16,512,128]{1,2,0:T(8,128)(2,1)}), bf16[16,512,128]{1,2,0:T(8,128)(2,1)}, u32[]{:S(2)}, u32[]{:S(2)}) %all-to-all-start.3) | async-done | bytes 2097184 | tf_op jit(solution)/shard_map/all_to_all | solution.py:18
  501.2 9.9 %all-to-all-start.4 = ((s32[16,1,8]{2,1,0:T(1,128)}), s32[16,1,8]{2,1,0:T(1,128)S(1)}, u32[]{:S(2)}, u32[]{:S(2)}) async-start(s32[16,1,8]{2,1,0:T(1,128)} %copy.87), calls=%async_computation.6 | async-start | bytes 16384 | tf_op jit(solution)/shard_map/all_to_all | solution.py:207
  521.3 23.5 %all_gather.16 = bf16[8,4096]{1,0:T(8,128)(2,1)S(1)} all-gather(bf16[8,256]{1,0:T(8,128)(2,1)S(1)} %get-tuple-element.84), channel_id=1, replica_groups=mesh['row'=16,'col'=16] {'col'}, dimensions={1}, use_global_device_ids=true | all-gather | bytes 69632 | tf_op jit(solution)/shard_map/all_gather | solution.py:163
  545.9 3.3 scatter_fusion.1
  549.3 14.1 %all-to-all-start.5 = ((bf16[16,8,4096]{2,1,0:T(8,128)(2,1)}), bf16[16,8,4096]{2,1,0:T(8,128)(2,1)S(1)}, u32[]{:S(2)}, u32[]{:S(2)}) async-start(bf16[16,8,4096]{2,1,0:T(8,128)(2,1)} %scatter_fusion.1), calls=%async_computation.7 | async-start | bytes 2097152 | tf_op jit(solution)/shard_map/all_to_all | solution.py:206
  563.5 18.9 %all-to-all-done.5 = bf16[16,8,4096]{2,1,0:T(8,128)(2,1)S(1)} async-done(((bf16[16,8,4096]{2,1,0:T(8,128)(2,1)}), bf16[16,8,4096]{2,1,0:T(8,128)(2,1)S(1)}, u32[]{:S(2)}, u32[]{:S(2)}) %all-to-all-start.5) | async-done | bytes 1048608 | tf_op jit(solution)/shard_map/all_to_all | solution.py:206
  585.6 23.9 %all_gather.18 = f32[16,8,32]{2,1,0:T(8,128)S(1)} all-gather(f32[1,8,32]{2,1,0:T(8,128)S(1)} %all_gather_reshape.10), channel_id=1, replica_groups=mesh['row'=16,'col'=16] {'col'}, dimensions={0}, use_global_device_ids=true | all-gather | bytes 17408 | tf_op jit(solution)/shard_map/all_gather | solution.py:27
  609.6 26.2 %all_gather.17 = f32[16,8,32]{2,1,0:T(8,128)S(1)} all-gather(f32[1,8,32]{2,1,0:T(8,128)S(1)} %all_gather_reshape.9), channel_id=1, replica_groups=mesh['row'=16,'col'=16] {'col'}, dimensions={0}, use_global_device_ids=true | all-gather | bytes 17408 | tf_op jit(solution)/shard_map/all_gather | solution.py:27
  649.9 7.3 all-gather.5.cloned.1.call-done
  661.1 16.8 %while.14 = (s32[]{:T(128)}, f32[8,32]{1,0:T(8,128)S(1)}, f32[8,32]{1,0:T(8,128)S(1)}, f32[8,32,128]{2,1,0:T(8,128)S(1)}, f32[15,8,32]{2,1,0:T(8,128)S(1)}, /*in...) while((s32[]{:T(128)}, f32[8,32]{1,0:T(8,128)S(1)}, f32[8,32]{1,0:T(8,128)S(1)}, ...), condition=%wide.region_20.21_spmd, body=%wide.region_19.20_spmd.sunk | while | flops 99842 | bytes 403549 | solution.py:30
  678.7 17.4 %all-to-all-start.7 = ((f32[16,8,2]{1,2,0:T(2,128)}), f32[16,8,2]{1,2,0:T(2,128)S(1)}, u32[]{:S(2)}, u32[]{:S(2)}) async-start(f32[16,8,2]{1,2,0:T(2,128)} %broadcast_in_dim.100), calls=%async_computation.9 | async-start | bytes 32768 | tf_op jit(solution)/shard_map/all_to_all | solution.py:237
  696.3 7.1 all-to-all-done.7
  704.0 3.7 all-to-all-start.8
  708.5 6.6 all-to-all-done.8
  715.8 3.7 all-to-all-start.6
  720.2 6.9 all-to-all-done.6
  (197 shorter events, 73.5 us)
Async XLA Ops:
  7.2 246.9 %copy-start = (bf16[1,384,2048]{2,1,0:T(8,128)(2,1)S(1)}, bf16[1,384,2048]{2,1,0:T(8,128)(2,1)}, u32[]{:S(2)}) copy-start(bf16[1,384,2048]{2,1,0:T(8,128)(2,1)} %param.28) | copy-start | bytes 4718596
  7.2 106.3 %reduce-scatter.3.cloned.1.call-start = ((), (), s32[]{:S(2)}) async-start(), calls=%async_computation.11 | async-start | bytes 4456448 | tf_op jit(solution)/shard_map/reduce_scatter | solution.py:98
  11.3 102.2 %copy-start.11 = (bf16[512,128]{1,0:T(8,128)(2,1)S(1)}, bf16[512,128]{1,0:T(8,128)(2,1)}, u32[]{:S(2)}) copy-start(bf16[512,128]{1,0:T(8,128)(2,1)} %param.20) | copy-start | bytes 393220
  116.1 7.1 copy-start.12
  116.1 8.8 %copy-start.19 = (s32[2]{0:T(128)S(1)}, s32[2]{0:T(128)}, u32[]{:S(2)}) copy-start(s32[2]{0:T(128)} %constant.155) | copy-start | bytes 28
  116.1 8.9 %copy-start.18 = (s32[2]{0:T(128)S(1)}, s32[2]{0:T(128)}, u32[]{:S(2)}) copy-start(s32[2]{0:T(128)} %constant.158) | copy-start | bytes 28
  116.1 40.0 %copy-start.15 = (bf16[2048]{0:T(1024)(128)(2,1)S(1)}, bf16[2048]{0:T(1024)(128)(2,1)}, u32[]{:S(2)}) copy-start(bf16[2048]{0:T(1024)(128)(2,1)} %param.22) | copy-start | bytes 12292
  116.1 55.1 %all-to-all-start = ((bf16[16,512,128]{2,1,0:T(8,128)(2,1)}), bf16[16,512,128]{2,1,0:T(8,128)(2,1)}, u32[]{:S(2)}, u32[]{:S(2)}) async-start(bf16[16,512,128]{2,1,0:T(8,128)(2,1)} %stack.6), calls=%async_computation.1 | async-start | bytes 4194304 | tf_op jit(solution)/shard_map/all_to_all | solution.py:18
  187.7 62.9 %copy-start.20 = (bf16[1,2048,384]{2,1,0:T(8,128)(2,1)S(1)}, bf16[1,2048,384]{2,1,0:T(8,128)(2,1)}, u32[]{:S(2)}) copy-start(bf16[1,2048,384]{2,1,0:T(8,128)(2,1)} %param.26) | copy-start | bytes 4718596
  263.7 5.7 copy-start.13
  263.7 61.3 %all-to-all-start.2 = ((bf16[16,64,2048]{2,1,0:T(8,128)(2,1)}), bf16[16,64,2048]{2,1,0:T(8,128)(2,1)}, u32[]{:S(2)}, u32[]{:S(2)}) async-start(bf16[16,64,2048]{2,1,0:T(8,128)(2,1)} %bitcast.199), calls=%async_computation.3 | async-start | bytes 8388608 | tf_op jit(solution)/shard_map/all_to_all | solution.py:137
  269.1 174.4 %reduce-scatter.5.cloned.1.call-start = ((), (), s32[]{:S(2)}) async-start(), calls=%async_computation.12 | async-start | bytes 4456448 | tf_op jit(solution)/shard_map/reduce_scatter | solution.py:146
  446.1 7.1 copy-start.16
  446.1 7.1 copy-start.22
  446.1 7.1 copy-start.17
  446.1 8.7 %copy-start.14 = (s32[1,504]{1,0:T(1,128)S(1)}, s32[1,504]{1,0:T(1,128)}, u32[]{:S(2)}) copy-start(s32[1,504]{1,0:T(1,128)} %param.31) | copy-start | bytes 6052
  446.1 55.0 %all-to-all-start.3 = ((bf16[16,512,128]{1,2,0:T(8,128)(2,1)}), bf16[16,512,128]{1,2,0:T(8,128)(2,1)}, u32[]{:S(2)}, u32[]{:S(2)}) async-start(bf16[16,512,128]{1,2,0:T(8,128)(2,1)} %stack.7), calls=%async_computation.5 | async-start | bytes 4194304 | tf_op jit(solution)/shard_map/all_to_all | solution.py:18
  501.2 48.1 %all-to-all-start.4 = ((s32[16,1,8]{2,1,0:T(1,128)}), s32[16,1,8]{2,1,0:T(1,128)S(1)}, u32[]{:S(2)}, u32[]{:S(2)}) async-start(s32[16,1,8]{2,1,0:T(1,128)} %copy.87), calls=%async_computation.6 | async-start | bytes 16384 | tf_op jit(solution)/shard_map/all_to_all | solution.py:207
  511.1 124.8 %all-gather.3.cloned.1.call-start = ((), (), s32[]{:S(2)}) async-start(), calls=%async_computation.13 | async-start | bytes 1114112 | tf_op jit(solution)/shard_map/all_gather | solution.py:162
  513.4 3.5 copy-start.8
  545.9 36.6 %copy-start.6 = (bf16[8,64,512]{2,1,0:T(8,128)(2,1)S(1)}, bf16[8,64,512]{2,1,0:T(8,128)(2,1)}, u32[]{:S(2)}) copy-start(bf16[8,64,512]{2,1,0:T(8,128)(2,1)} %param.34) | copy-start | bytes 1572868
  549.2 33.8 %copy-start.21 = (bf16[8,64,512]{2,1,0:T(8,128)(2,1)S(1)}, bf16[8,64,512]{2,1,0:T(8,128)(2,1)}, u32[]{:S(2)}) copy-start(bf16[8,64,512]{2,1,0:T(8,128)(2,1)} %param.35) | copy-start | bytes 1572868
  549.3 33.2 %all-to-all-start.5 = ((bf16[16,8,4096]{2,1,0:T(8,128)(2,1)}), bf16[16,8,4096]{2,1,0:T(8,128)(2,1)S(1)}, u32[]{:S(2)}, u32[]{:S(2)}) async-start(bf16[16,8,4096]{2,1,0:T(8,128)(2,1)} %scatter_fusion.1), calls=%async_computation.7 | async-start | bytes 2097152 | tf_op jit(solution)/shard_map/all_to_all | solution.py:206
  563.4 93.8 %all-gather.5.cloned.1.call-start = ((), (), s32[]{:S(2)}) async-start(), calls=%async_computation.14 | async-start | bytes 2228224 | tf_op jit(solution)/shard_map/all_gather | solution.py:27
  609.6 28.8 %copy-start.9 = (f32[16,8,32]{2,1,0:T(8,128)}, f32[16,8,32]{2,1,0:T(8,128)S(1)}, u32[]{:S(2)}) copy-start(f32[16,8,32]{2,1,0:T(8,128)S(1)} %all_gather.18) | copy-start | bytes 49156
  642.5 4.3 copy-start.4
  649.9 11.2 %slice-start = ((f32[16,8,32]{2,1,0:T(8,128)}), f32[15,8,32]{2,1,0:T(8,128)S(1)}, s32[]{:S(2)}) async-start(f32[16,8,32]{2,1,0:T(8,128)} %copy-done.9), calls=%async_computation.15 | async-start | bytes 122880 | tf_op jit(solution)/shard_map/slice | solution.py:29
  649.9 11.2 %slice-start.1 = ((f32[16,8,32]{2,1,0:T(8,128)}), f32[15,8,32]{2,1,0:T(8,128)S(1)}, s32[]{:S(2)}) async-start(f32[16,8,32]{2,1,0:T(8,128)} %copy-done.10), calls=%async_computation.16 | async-start | bytes 122880 | tf_op jit(solution)/shard_map/slice | solution.py:29
  661.1 67.8 %copy-start.1 = (bf16[1,384,2048]{2,1,0:T(8,128)(2,1)S(1)}, bf16[1,384,2048]{2,1,0:T(8,128)(2,1)}, u32[]{:S(2)}) copy-start(bf16[1,384,2048]{2,1,0:T(8,128)(2,1)} %param.28) | copy-start | bytes 4718596
  678.7 24.7 %all-to-all-start.7 = ((f32[16,8,2]{1,2,0:T(2,128)}), f32[16,8,2]{1,2,0:T(2,128)S(1)}, u32[]{:S(2)}, u32[]{:S(2)}) async-start(f32[16,8,2]{1,2,0:T(2,128)} %broadcast_in_dim.100), calls=%async_computation.9 | async-start | bytes 32768 | tf_op jit(solution)/shard_map/all_to_all | solution.py:237
  704.0 11.0 %all-to-all-start.8 = ((f32[16,8,2]{1,2,0:T(2,128)}), f32[16,8,2]{1,2,0:T(2,128)S(1)}, u32[]{:S(2)}, u32[]{:S(2)}) async-start(f32[16,8,2]{1,2,0:T(2,128)} %broadcast_in_dim.101), calls=%async_computation.10 | async-start | bytes 32768 | tf_op jit(solution)/shard_map/all_to_all | solution.py:238
  715.8 11.4 %all-to-all-start.6 = ((f32[16,8,2,128]{3,2,1,0:T(2,128)}), f32[16,8,2,128]{3,2,1,0:T(2,128)S(1)}, u32[]{:S(2)}, u32[]{:S(2)}) async-start(f32[16,8,2,128]{3,2,1,0:T(2,128)} %broadcast_in_dim.99), calls=%async_computation.8 | async-start | bytes 262144 | tf_op jit(solution)/shard_map/all_to_all | solution.py:239
  (5 other events, 8.6 us)
Sparse Core Ops, SparseCore 0:
  11.4 101.9 reduce-scatter.2
  348.0 95.4 reduce-scatter.4
  518.2 64.8 all-gather.2
  584.8 72.2 all-gather.4
